TPU v7x, 32 devices: a whole 2x2x4 slice. The times are simulated.
32 devices in a mesh: dp: 16 (over z, y, core), tensor: 2 (over x).
Axes of the slice: x: 2, y: 2, z: 4, core: 2. Of those that a mesh axis runs over, the one named last changes fastest.
Arguments:
- patches: bfloat16 [50176, 768], P(('dp', 'tensor')), may hold values from -6 to 6
- visible: int32 [1024, 49], P(('dp', 'tensor')), may hold values from 0 to 195, as said below
- pos_table: float32 [196, 768], replicated, may hold values from -6 to 6
- cotangent: bfloat16 [50176, 768], P(('dp', 'tensor')), may hold values from -6 to 6
- step_count: int32 [1], replicated, may hold values from 2 to 20
- w_qkv: float32 [768, 3, 768], P('dp', None, 'tensor'), may hold values from -0.21875 to 0.21875
- m_qkv: float32 [768, 3, 768], P('dp', None, 'tensor'), may hold values from -0.00018793954 to 0.00018793954
- v_qkv: float32 [768, 3, 768], P('dp', None, 'tensor'), may hold values from 7.48811e-09 to 2.9669868e-08
- w_proj: float32 [768, 768], P('tensor', 'dp'), may hold values from -0.875 to 0.875
- m_proj: float32 [768, 768], P('tensor', 'dp'), may hold values from -0.00018793954 to 0.00018793954
- v_proj: float32 [768, 768], P('tensor', 'dp'), may hold values from 7.48811e-09 to 2.9669868e-08
- w_fc1: float32 [768, 4, 768], P('dp', None, 'tensor'), may hold values from -0.21875 to 0.21875
- m_fc1: float32 [768, 4, 768], P('dp', None, 'tensor'), may hold values from -0.00018793954 to 0.00018793954
- v_fc1: float32 [768, 4, 768], P('dp', None, 'tensor'), may hold values from 7.48811e-09 to 2.9669868e-08
- w_fc2: float32 [4, 768, 768], P(None, 'tensor', 'dp'), may hold values from -0.109375 to 0.109375
- m_fc2: float32 [4, 768, 768], P(None, 'tensor', 'dp'), may hold values from -0.00018793954 to 0.00018793954
- v_fc2: float32 [4, 768, 768], P(None, 'tensor', 'dp'), may hold values from 7.48811e-09 to 2.9669868e-08
- split_bias: float32 [6, 768], P(None, 'tensor'), may hold values from -3 to 3
- m_split: float32 [6, 768], P(None, 'tensor'), may hold values from -0.0005638186 to 0.0005638186
- v_split: float32 [6, 768], P(None, 'tensor'), may hold values from 6.640399e-08 to 2.6844165e-07
- norm_bias: float32 [6, 768], replicated, may hold values from -1.2 to 1.8
- m_norm: float32 [6, 768], replicated, may hold values from -0.0005638186 to 0.0005638186
- v_norm: float32 [6, 768], replicated, may hold values from 6.640399e-08 to 2.6844165e-07
Outputs:
- block_out: bfloat16 [50176, 768], P(('dp', 'tensor'))
- input_grad: float32 [50176, 768], P(('dp', 'tensor'))
- grad_norm: float32 [], replicated
- new_qkv: float32 [768, 3, 768], P('dp', None, 'tensor')
- first_qkv: float32 [768, 3, 768], P('dp', None, 'tensor')
- second_qkv: float32 [768, 3, 768], P('dp', None, 'tensor')
- new_proj: float32 [768, 768], P('tensor', 'dp')
- first_proj: float32 [768, 768], P('tensor', 'dp')
- second_proj: float32 [768, 768], P('tensor', 'dp')
- new_fc1: float32 [768, 4, 768], P('dp', None, 'tensor')
- first_fc1: float32 [768, 4, 768], P('dp', None, 'tensor')
- second_fc1: float32 [768, 4, 768], P('dp', None, 'tensor')
- new_fc2: float32 [4, 768, 768], P(None, 'tensor', 'dp')
- first_fc2: float32 [4, 768, 768], P(None, 'tensor', 'dp')
- second_fc2: float32 [4, 768, 768], P(None, 'tensor', 'dp')
- new_split: float32 [6, 768], P(None, 'tensor')
- first_split: float32 [6, 768], P(None, 'tensor')
- second_split: float32 [6, 768], P(None, 'tensor')
- new_norm: float32 [6, 768], replicated
- first_norm: float32 [6, 768], replicated
- second_norm: float32 [6, 768], replicated
Inputs may be any that keep to these rules, and one draw needn't show every extreme that they name: `visible`: the 49 entries of an image are distinct patch positions.
All inputs are finite; a program needn't handle non-finite values.
Results may differ from a plain program's by a relative error of at most 0.014.
Values may be sent and summed in bfloat16 or wider, within the bound.
No kernel may reach another device: no remote copies, remote signals or barrier semaphores. Data moves between devices by JAX's collectives and lax.ppermute only.
A program may use at most 256 MiB of HBM per device.

v0:
```python
import jax
import jax.numpy as jnp
from jax import lax
from jax.sharding import PartitionSpec as P

HD = 64
VISIBLE = 49
norm_eps = 1e-06
beta_one = 0.9
beta_two = 0.95
adam_eps = 1e-08
clip_value = 1.0
matrix_rate = 0.02
proj_rate = 0.08
vector_rate = 0.2
matrix_decay = 0.05


def layer_norm(values, row_gain, row_shift):
    row_mean = jnp.mean(values, axis=-1, keepdims=True)
    centred = values - row_mean
    variance = jnp.mean(centred * centred, axis=-1, keepdims=True)
    return centred * lax.rsqrt(variance + norm_eps) * row_gain + row_shift


def adam_update(
    weight, gradient, first_moment, second, factor, bias_first, bias_second, learn_rate, decay_rate
):
    clipped = gradient * factor
    first_new = beta_one * first_moment + (1.0 - beta_one) * clipped
    second_new = beta_two * second + (1.0 - beta_two) * clipped * clipped
    direction = first_new / bias_first / (jnp.sqrt(second_new / bias_second) + adam_eps)
    return (weight - learn_rate * (direction + decay_rate * weight), first_new, second_new)


def transpose_dot(left_side, right_side):
    return lax.dot_general(
        left_side, right_side, (((0,), (0,)), ((), ())), preferred_element_type=jnp.float32
    )


def dot_back(left_side, right_side):
    return lax.dot_general(
        left_side, right_side, (((1,), (1,)), ((), ())), preferred_element_type=jnp.float32
    )


def square_sum(arrays):
    total = jnp.sum(arrays[0] * arrays[0])
    for member in arrays[1:]:
        total = total + jnp.sum(member * member)
    return total


def standard_normal(values):
    cumulative = 0.5 + 0.5 * lax.erf(values * 0.5**0.5)
    density = jnp.exp(-0.5 * values * values) * (0.5 / jnp.pi) ** 0.5
    return (cumulative, density)


def body(
    patches,
    visible,
    pos_table,
    cotangent,
    step_count,
    w_qkv,
    m_qkv,
    v_qkv,
    w_proj,
    m_proj,
    v_proj,
    w_fc1,
    m_fc1,
    v_fc1,
    w_fc2,
    m_fc2,
    v_fc2,
    split_bias,
    m_split,
    v_split,
    norm_bias,
    m_norm,
    v_norm,
):
    model_width = patches.shape[1]
    shard_rows = w_qkv.shape[0]
    shard_width = w_qkv.shape[2]
    halves = model_width // shard_width
    attn_scale = HD ** (-0.5)
    full_rows = patches.shape[0]
    every = ("tensor", "dp")
    low_type = jnp.bfloat16

    def rows_of(proj_like):
        return jnp.swapaxes(proj_like, -1, -2)

    def gather(block):
        whole = lax.all_gather(block.astype(low_type), every, axis=0, tiled=True)
        return whole.reshape(halves, model_width, block.shape[1])

    fc2_rows = jnp.transpose(w_fc2, (2, 0, 1)).reshape(shard_rows, 4 * shard_width)
    qkv_low = gather(w_qkv.reshape(shard_rows, 3 * shard_width))
    rest_low = gather(
        jnp.concatenate(
            [rows_of(w_proj), w_fc1.reshape(shard_rows, 4 * shard_width), fc2_rows], axis=1
        )
    )
    proj_low = [rest_low[t, :, :shard_width] for t in range(halves)]
    fc1_low = [rest_low[t, :, shard_width : 5 * shard_width] for t in range(halves)]
    fc2_low = [rest_low[t, :, 5 * shard_width :] for t in range(halves)]
    split_whole_bias = lax.all_gather(split_bias, "tensor", axis=0, tiled=False)
    inputs = patches.astype(jnp.float32) + jnp.take(pos_table, visible.reshape(-1), axis=0)
    normed, norm_back = jax.vjp(layer_norm, inputs, norm_bias[0], norm_bias[1])
    normed_low = normed.astype(low_type)
    heads_here = shard_width // HD
    head_shape = (full_rows // VISIBLE, VISIBLE, heads_here, HD)
    attended = jnp.zeros((full_rows, model_width), jnp.float32)
    kept = []
    for t in range(halves):
        projected = jnp.dot(normed_low, qkv_low[t], preferred_element_type=jnp.float32)
        bias_t = split_whole_bias[t]
        query_heads = (projected[:, :shard_width] + bias_t[0]).astype(low_type).reshape(head_shape)
        key_heads = projected[:, shard_width : 2 * shard_width].astype(low_type).reshape(head_shape)
        value_heads = (
            (projected[:, 2 * shard_width :] + bias_t[1]).astype(low_type).reshape(head_shape)
        )
        scores = (
            jnp.einsum(
                "bqhd,bkhd->bhqk", query_heads, key_heads, preferred_element_type=jnp.float32
            )
            * attn_scale
        )
        attention = jax.nn.softmax(scores, axis=-1)
        soft_low = attention.astype(low_type)
        mixed_low = (
            jnp.einsum("bhqk,bkhd->bqhd", soft_low, value_heads, preferred_element_type=jnp.float32)
            .reshape(full_rows, shard_width)
            .astype(low_type)
        )
        attended = attended + dot_back(mixed_low, proj_low[t])
        kept.append((query_heads, key_heads, value_heads, attention, soft_low, mixed_low))
    hidden_res = inputs + (attended + norm_bias[2])
    normed_two, norm_two_back = jax.vjp(layer_norm, hidden_res, norm_bias[3], norm_bias[4])
    normed_two_low = normed_two.astype(low_type)
    ffn_out = jnp.zeros((full_rows, model_width), jnp.float32)
    grad_out = cotangent.astype(jnp.float32)
    grad_normed_two = jnp.zeros((full_rows, model_width), jnp.float32)
    grad_fc1, grad_fc2, grad_fc1_bias = ([], [], [])
    for t in range(halves):
        pre_gelu = jnp.dot(
            normed_two_low, fc1_low[t], preferred_element_type=jnp.float32
        ) + split_whole_bias[t, 2:].reshape(-1)
        cumulative, density = standard_normal(pre_gelu)
        activated_low = (pre_gelu * cumulative).astype(low_type)
        slope_low = (cumulative + pre_gelu * density).astype(low_type)
        ffn_out = ffn_out + dot_back(activated_low, fc2_low[t])
        grad_fc2.append(transpose_dot(cotangent, activated_low).astype(low_type))
        grad_act = jnp.dot(cotangent, fc2_low[t], preferred_element_type=jnp.float32)
        grad_pre = (grad_act * slope_low.astype(jnp.float32)).astype(low_type)
        grad_fc1.append(transpose_dot(normed_two_low, grad_pre).astype(low_type))
        grad_fc1_bias.append(jnp.sum(grad_pre.astype(jnp.float32), axis=0).reshape(4, shard_width))
        grad_normed_two = grad_normed_two + dot_back(grad_pre, fc1_low[t])
    block_out = (hidden_res + (ffn_out + norm_bias[5])).astype(low_type)

    def scatter(parts):
        stacked = jnp.stack(parts).reshape(halves * model_width, parts[0].shape[1])
        return lax.psum_scatter(stacked, every, scatter_dimension=0, tiled=True).astype(jnp.float32)

    ffn_shard = scatter(
        [jnp.concatenate([grad_fc1[t], grad_fc2[t]], axis=1) for t in range(halves)]
    )
    grad_hidden_norm, grad_gain_two, grad_shift_two = norm_two_back(grad_normed_two)
    grad_hidden = grad_out + grad_hidden_norm
    grad_attn_low = grad_hidden.astype(low_type)
    grad_normed = jnp.zeros((full_rows, model_width), jnp.float32)
    grad_front, grad_query_bias = ([], [])
    for t in range(halves):
        query_heads, key_heads, value_heads, attention, soft_low, mixed_low = kept[t]
        grad_proj = transpose_dot(grad_attn_low, mixed_low).astype(low_type)
        grad_mixed = (
            jnp.dot(grad_attn_low, proj_low[t], preferred_element_type=jnp.float32)
            .astype(low_type)
            .reshape(head_shape)
        )
        grad_soft = jnp.einsum(
            "bqhd,bkhd->bhqk", grad_mixed, value_heads, preferred_element_type=jnp.float32
        )
        grad_values = jnp.einsum(
            "bhqk,bqhd->bkhd", soft_low, grad_mixed, preferred_element_type=jnp.float32
        ).astype(low_type)
        grad_scores = (
            attention * (grad_soft - jnp.sum(grad_soft * attention, axis=-1, keepdims=True))
        ).astype(low_type)
        grad_queries = (
            jnp.einsum(
                "bhqk,bkhd->bqhd", grad_scores, key_heads, preferred_element_type=jnp.float32
            )
            * attn_scale
        ).astype(low_type)
        grad_keys = (
            jnp.einsum(
                "bhqk,bqhd->bkhd", grad_scores, query_heads, preferred_element_type=jnp.float32
            )
            * attn_scale
        ).astype(low_type)
        grad_query_rows = grad_queries.reshape(full_rows, shard_width)
        grad_value_rows = grad_values.reshape(full_rows, shard_width)
        grad_proj_in = jnp.concatenate(
            [grad_query_rows, grad_keys.reshape(full_rows, shard_width), grad_value_rows], axis=1
        )
        grad_qkv = transpose_dot(normed_low, grad_proj_in).astype(low_type)
        grad_front.append(jnp.concatenate([grad_qkv, grad_proj], axis=1))
        grad_normed = grad_normed + dot_back(grad_proj_in, qkv_low[t])
        grad_query_bias.append(
            jnp.stack(
                [
                    jnp.sum(grad_query_rows.astype(jnp.float32), axis=0),
                    jnp.sum(grad_value_rows.astype(jnp.float32), axis=0),
                ]
            )
        )
    front_shard = scatter(grad_front)
    grad_input_norm, grad_gain_one, grad_shift_one = norm_back(grad_normed)
    input_grad = grad_hidden + grad_input_norm
    grad_split = jnp.stack(
        [jnp.concatenate([grad_query_bias[t], grad_fc1_bias[t]]) for t in range(halves)]
    )
    grad_norm_rows = jnp.stack(
        [
            grad_gain_one,
            grad_shift_one,
            jnp.sum(grad_attn_low.astype(jnp.float32), axis=0),
            grad_gain_two,
            grad_shift_two,
            jnp.sum(grad_out, axis=0),
        ]
    )
    shards = (
        front_shard[:, : 3 * shard_width].reshape(shard_rows, 3, shard_width),
        rows_of(front_shard[:, 3 * shard_width :]),
        ffn_shard[:, : 4 * shard_width].reshape(shard_rows, 4, shard_width),
        jnp.transpose(
            ffn_shard[:, 4 * shard_width :].reshape(shard_rows, 4, shard_width), (1, 2, 0)
        ),
    )
    local_square = square_sum((front_shard, ffn_shard))
    norm_total, split_whole, square_total = lax.psum(
        (grad_norm_rows, grad_split, local_square), ("dp", "tensor")
    )
    split_total = split_whole[lax.axis_index("tensor")]
    grad_norm = jnp.sqrt(
        square_total + jnp.sum(norm_total * norm_total) + jnp.sum(split_whole * split_whole)
    )
    factor = jnp.minimum(1.0, clip_value / (grad_norm + 1e-06))
    step_value = step_count[0].astype(jnp.float32)
    bias_first = 1.0 - jnp.power(beta_one, step_value)
    bias_second = 1.0 - jnp.power(beta_two, step_value)
    qkv_out = adam_update(
        w_qkv, shards[0], m_qkv, v_qkv, factor, bias_first, bias_second, matrix_rate, matrix_decay
    )
    proj_out = adam_update(
        w_proj, shards[1], m_proj, v_proj, factor, bias_first, bias_second, proj_rate, matrix_decay
    )
    fc1_out = adam_update(
        w_fc1, shards[2], m_fc1, v_fc1, factor, bias_first, bias_second, matrix_rate, matrix_decay
    )
    fc2_out = adam_update(
        w_fc2, shards[3], m_fc2, v_fc2, factor, bias_first, bias_second, matrix_rate, matrix_decay
    )
    split_out = adam_update(
        split_bias, split_total, m_split, v_split, factor, bias_first, bias_second, vector_rate, 0.0
    )
    norm_out = adam_update(
        norm_bias, norm_total, m_norm, v_norm, factor, bias_first, bias_second, vector_rate, 0.0
    )
    return (
        block_out,
        input_grad,
        grad_norm,
        qkv_out[0],
        qkv_out[1],
        qkv_out[2],
        proj_out[0],
        proj_out[1],
        proj_out[2],
        fc1_out[0],
        fc1_out[1],
        fc1_out[2],
        fc2_out[0],
        fc2_out[1],
        fc2_out[2],
        split_out[0],
        split_out[1],
        split_out[2],
        norm_out[0],
        norm_out[1],
        norm_out[2],
    )


def solution(mesh):
    return jax.shard_map(
        body,
        mesh=mesh,
        in_specs=(
            P(("dp", "tensor"), None),
            P(("dp", "tensor"), None),
            P(),
            P(("dp", "tensor"), None),
            P(),
            P("dp", None, "tensor"),
            P("dp", None, "tensor"),
            P("dp", None, "tensor"),
            P("tensor", "dp"),
            P("tensor", "dp"),
            P("tensor", "dp"),
            P("dp", None, "tensor"),
            P("dp", None, "tensor"),
            P("dp", None, "tensor"),
            P(None, "tensor", "dp"),
            P(None, "tensor", "dp"),
            P(None, "tensor", "dp"),
            P(None, "tensor"),
            P(None, "tensor"),
            P(None, "tensor"),
            P(),
            P(),
            P(),
        ),
        out_specs=(
            P(("dp", "tensor"), None),
            P(("dp", "tensor"), None),
            P(),
            P("dp", None, "tensor"),
            P("dp", None, "tensor"),
            P("dp", None, "tensor"),
            P("tensor", "dp"),
            P("tensor", "dp"),
            P("tensor", "dp"),
            P("dp", None, "tensor"),
            P("dp", None, "tensor"),
            P("dp", None, "tensor"),
            P(None, "tensor", "dp"),
            P(None, "tensor", "dp"),
            P(None, "tensor", "dp"),
            P(None, "tensor"),
            P(None, "tensor"),
            P(None, "tensor"),
            P(),
            P(),
            P(),
        ),
        check_vma=False,
    )
```

profile of v0, /device:TPU:0, one launch (start us, length us, event | category | flops | bytes accessed | tf_op | source)
XLA Modules:
  0.0 661.8 jit_solution(4477941152413452380)
XLA Ops:
  14.5 5.6 all-gather.1
  20.2 6.1 gather_fusion
  27.0 3.5 fusion.107
  33.8 40.4 %all-gather.5.cloned.1.call-done = bf16[1536,1152]{1,0:T(8,128)(2,1)} async-done(((bf16[48,1152]{1,0:T(8,128)(2,1)}), bf16[1536,1152]{1,0:T(8,128)(2,1)}) %all-gather.5.cloned.1.call-update) | async-done | bytes 3538960 | tf_op jit(solution)/shard_map/all_gather | solution.py:99
  74.2 4.8 fusion.68
  83.1 4.9 reshape.281
  88.0 5.7 fusion.72
  97.5 4.8 reshape.280
  102.3 3.2 reshape.275
  105.5 4.7 reshape.279
  110.2 3.7 reshape.273
  113.9 3.8 reshape.274
  117.7 4.7 fusion.53
  122.4 8.9 %fusion.109 = (f32[32,6,49]{2,1,0:T(8,128)S(1)}, f32[32,6,49,49]{2,3,1,0:T(8,128)S(1)}) fusion(f32[32,6,49,49]{2,3,1,0:T(8,128)S(1)} %fusion.53), kind=kOutput, calls=%fused_computation.231 | output fusion | flops 1844016 | bytes 3725568 | tf_op jit(solution)/shard_map/sub | solution.py:134
  137.8 5.2 convert_element_type.213
  143.0 3.5 fusion.45
  146.5 8.9 %fusion.110 = (f32[32,6,49]{2,1,0:T(8,128)S(1)}, f32[32,6,49,49]{2,3,1,0:T(8,128)S(1)}) fusion(f32[32,6,49,49]{2,3,1,0:T(8,128)S(1)} %fusion.45), kind=kOutput, calls=%fused_computation.232 | output fusion | flops 1844016 | bytes 3725568 | tf_op jit(solution)/shard_map/sub | solution.py:134
  160.2 4.6 convert_element_type.219
  167.6 3.2 fusion.111
  174.1 8.7 %multiply_convert_fusion = (bf16[1568,1536]{1,0:T(8,128)(2,1)}, f32[1568,1536]{1,0:T(8,128)}) fusion(f32[1536]{0:T(1024)S(1)} %add.329, bf16[1568,768]{1,0:T(8,128)(2,1)S(1)} %add_convert_fusion.1, bf16[2,768,3456]{2,1,0:T(8,128)(2,1)S(1)} %bitcast.204), kind=kOutput, calls=%fused_computation.21 | convolution fusion | flops 3713826816 | bytes 19226624 | tf_op jit(solution)/shard_map/dot_general | solution.py:151
  182.9 8.8 %multiply_convert_fusion.1 = (bf16[1568,1536]{1,0:T(8,128)(2,1)}, f32[1568,1536]{1,0:T(8,128)}) fusion(f32[1536]{0:T(1024)S(1)} %add.325, bf16[1568,768]{1,0:T(8,128)(2,1)S(1)} %add_convert_fusion.1, bf16[2,768,3456]{2,1,0:T(8,128)(2,1)S(1)} %bitcast.205), kind=kOutput, calls=%fused_computation.23 | convolution fusion | flops 3713826816 | bytes 19226624 | tf_op jit(solution)/shard_map/dot_general | solution.py:151
  191.7 11.1 %convert_reduce_fusion = (f32[1536]{0:T(1024)}, bf16[1568,1536]{1,0:T(8,128)(2,1)}) fusion(f32[1568,1536]{1,0:T(8,128)} %get-tuple-element.127, bf16[1568,768]{1,0:T(8,128)(2,1)S(1)} %copy-done.14, bf16[2,768,3456]{2,1,0:T(8,128)(2,1)S(1)} %bitcast.206), kind=kOutput, calls=%fused_computation.19 | convolution fusion | flops 3733092864 | bytes 19224576 | tf_op jit(solution)/shard_map/dot_general | solution.py:159
  202.8 9.4 %convert_reduce_fusion.1 = (f32[1536]{0:T(1024)}, bf16[1568,1536]{1,0:T(8,128)(2,1)S(1)}) fusion(f32[1568,1536]{1,0:T(8,128)} %get-tuple-element.125, bf16[1568,768]{1,0:T(8,128)(2,1)S(1)} %copy-done.14, bf16[2,768,3456]{2,1,0:T(8,128)(2,1)S(1)} %bitcast.207), kind=kOutput, calls=%fused_computation.20 | convolution fusion | flops 3733092864 | bytes 19224576 | tf_op jit(solution)/shard_map/dot_general | solution.py:159
  212.2 5.7 fusion.65
  218.0 9.9 %multiply_reduce_fusion.4 = (f32[768]{0:T(1024)S(1)}, f32[1568]{0:T(1024)S(1)}, f32[768]{0:T(1024)S(1)}, f32[1568,768]{1,0:T(8,128)S(1)}) fusion(f32[1568,768]{1,0:T(8,128)S(1)} %get-tuple-element.123, f32[1568]{0:T(1024)S(1)} %fusion.91, f32[1568]{0:T(1024)S(1)} %broadcast_multiply_fusion, f32[768]{0:T(1024)S(1)} %get-tuple-element.71, ...), kind=kOutput, calls=%fused_computation.50 | convolution fusion | flops 3710211072 | bytes 21654912 | tf_op jit(solution)/shard_map/dot_general | solution.py:43
  236.7 3.5 convolution_convert_fusion.6
  242.8 5.2 reshape.286
  248.0 6.5 multiply_reduce_fusion
  254.6 3.1 convert_reduce_fusion.3
  259.7 3.2 fusion.26
  262.9 3.3 convert_reduce_fusion.4
  266.1 3.3 reshape.282
  269.5 6.5 multiply_reduce_fusion.1
  284.2 3.2 convert_reduce_fusion.6
  314.7 7.0 %convolution_convert_fusion.1 = bf16[768,1152]{1,0:T(8,128)(2,1)} fusion(bf16[1568,768]{1,0:T(8,128)(2,1)S(1)} %copy-done.27, bf16[1568,1152]{1,0:T(8,128)(2,1)} %constant_dynamic-update-slice_fusion), kind=kOutput, calls=%fused_computation.69 | convolution fusion | flops 2775416832 | bytes 7790592 | tf_op jit(solution)/shard_map/dot_general | solution.py:37
  338.1 5.9 convolution_convert_fusion
  348.4 7.8 %convolution_convert_fusion.3 = bf16[768,1536]{1,0:T(8,128)(2,1)S(1)} fusion(bf16[1568,768]{1,0:T(8,128)(2,1)} %copy-done.29, bf16[1568,1536]{1,0:T(8,128)(2,1)} %get-tuple-element.135), kind=kOutput, calls=%fused_computation.71 | convolution fusion | flops 3700555776 | bytes 9584640 | tf_op jit(solution)/shard_map/dot_general | solution.py:37
  356.2 7.3 %fusion.22 = bf16[768,1536]{1,0:T(8,128)(2,1)S(1)} fusion(bf16[1568,1536]{1,0:T(8,128)(2,1)} %get-tuple-element.126, bf16[1568,768]{1,0:T(8,128)(2,1)S(1)} %copy-done.15), kind=kOutput, calls=%fused_computation.76 | convolution fusion | flops 3700555776 | bytes 9584640 | tf_op jit(solution)/shard_map/dot_general | solution.py:37
  366.5 4.8 convolution_convert_fusion.5
  371.4 5.0 fusion.21
  379.1 8.5 %pad_maximum_fusion = bf16[2,768,3072]{2,1,0:T(8,128)(2,1)} fusion(bf16[1,768,3072]{2,1,0:T(8,128)(2,1)} %maximum_bitcast_fusion.1, bf16[1,768,3072]{2,1,0:T(8,128)(2,1)} %maximum_bitcast_fusion), kind=kLoop, calls=%fused_computation.25 | loop fusion | flops 4718592 | bytes 18874368 | tf_op jit(solution)/shard_map/stack | solution.py:167
  388.8 8.3 %fusion.70 = f32[1568,768]{1,0:T(8,128)} fusion(bf16[1568,1152]{1,0:T(8,128)(2,1)} %constant_dynamic-update-slice_fusion, bf16[1536,1152]{1,0:T(8,128)(2,1)} %all-gather.5.cloned.1.call-done), kind=kOutput, calls=%fused_computation.136 | convolution fusion | flops 2774532096 | bytes 10199040 | tf_op jit(solution)/shard_map/dot_general | solution.py:43
  397.2 7.0 %multiply_reduce_fusion.5 = (f32[768]{0:T(1024)S(1)}, f32[1568]{0:T(1024)S(1)}, f32[768]{0:T(1024)S(1)}, f32[1568,768]{1,0:T(8,128)S(1)}) fusion(f32[1568,768]{1,0:T(8,128)S(1)} %bitcast.176, f32[1568]{0:T(1024)S(1)} %copy-done.50, f32[1568]{0:T(1024)S(1)} %copy-done.42, f32[768]{0:T(1024)S(1)} %copy-done.54, f32[1568,768]{1,0:T(8,128)} %fusion.70, ...), kind=kOutput, calls=%fused_computation.52 | convolution fusion | flops 2785367040 | bytes 19865728 | tf_op jit(solution)/shard_map/dot_general | solution.py:43
  409.1 7.0 %fusion.66 = f32[1568,768]{1,0:T(8,128)S(1)} fusion(bf16[1568,1536]{1,0:T(8,128)(2,1)} %get-tuple-element.124, bf16[2,768,3456]{2,1,0:T(8,128)(2,1)} %bitcast.200), kind=kOutput, calls=%fused_computation.132 | convolution fusion | flops 3699376128 | bytes 11993088 | tf_op jit(solution)/shard_map/dot_general | solution.py:43
  416.1 8.7 %add_convert_fusion = bf16[1568,768]{1,0:T(8,128)(2,1)} fusion(f32[1568,768]{1,0:T(8,128)S(1)} %bitcast.178, f32[1568,768]{1,0:T(8,128)S(1)} %fusion.66, bf16[1568,1536]{1,0:T(8,128)(2,1)} %get-tuple-element.126, f32[768]{0:T(1024)S(1)} %copy-done.57, bf16[2,768,3456]{2,1,0:T(8,128)(2,1)} %bitcast.201), kind=kOutput, calls=%fused_computation.56 | convolution fusion | flops 3704193024 | bytes 19221504 | tf_op jit(solution)/shard_map/dot_general | solution.py:43
  424.8 29.5 %reduce-scatter.3.cloned.1.call-done = bf16[48,1536]{1,0:T(8,128)(2,1)} async-done(((bf16[1536,1536]{1,0:T(8,128)(2,1)}), bf16[48,1536]{1,0:T(8,128)(2,1)}) %reduce-scatter.3.cloned.1.call-update) | async-done | bytes 147472 | tf_op jit(solution)/shard_map/reduce_scatter | solution.py:168
  455.9 139.4 %reduce-scatter.5.cloned.1.call-done = bf16[48,3072]{1,0:T(8,128)(2,1)} async-done(((bf16[1536,3072]{1,0:T(8,128)(2,1)}), bf16[48,3072]{1,0:T(8,128)(2,1)}) %reduce-scatter.5.cloned.1.call-update) | async-done | bytes 294928 | tf_op jit(solution)/shard_map/reduce_scatter | solution.py:168
  599.2 40.4 %all-reduce = (f32[]{:T(128)}, f32[6,768]{1,0:T(8,128)S(1)}, f32[2,6,384]{2,1,0:T(8,128)S(1)}) all-reduce(f32[]{:T(128)S(6)} %add.344, f32[6,768]{1,0:T(8,128)S(1)} %stack.60, f32[2,6,384]{2,1,0:T(8,128)S(1)} %pad_maximum_fusion.3), channel_id=1, replica_groups=mesh['dp'=16,'tensor'=2] {'dp','tensor'}, use_global_device_ids=true, to_apply=%region_18.19 | all-reduce | flops 9217 | bytes 73736 | tf_op jit(solution)/shard_map/psum | solution.py:248
  (284 shorter events, 133.2 us)
Async XLA Ops:
  7.2 13.0 %copy-start = (f32[196,768]{1,0:T(8,128)S(1)}, f32[196,768]{1,0:T(8,128)}, u32[]{:S(2)}) copy-start(f32[196,768]{1,0:T(8,128)} %param.25) | copy-start | bytes 1806340
  7.2 66.9 %all-gather.5.cloned.1.call-start = ((), (), s32[]{:S(2)}) async-start(), calls=%async_computation.2 | async-start | bytes 3649536 | tf_op jit(solution)/shard_map/all_gather | solution.py:99
  8.9 155.9 %all-gather.7.cloned.1.call-start = ((), (), s32[]{:S(2)}) async-start(), calls=%async_computation.3 | async-start | bytes 10948608 | tf_op jit(solution)/shard_map/all_gather | solution.py:99
  12.8 441.6 %reduce-scatter.3.cloned.1.call-start = ((), (), s32[]{:S(2)}) async-start(), calls=%async_computation.4 | async-start | bytes 4866048 | tf_op jit(solution)/shard_map/reduce_scatter | solution.py:168
  20.2 6.8 %copy-start.25 = (bf16[1568,768]{1,0:T(8,128)(2,1)S(1)}, bf16[1568,768]{1,0:T(8,128)(2,1)}, u32[]{:S(2)}) copy-start(bf16[1568,768]{1,0:T(8,128)(2,1)} %param.23) | copy-start | bytes 7225348
  33.8 45.2 %copy-start.26 = (bf16[1568,768]{1,0:T(8,128)(2,1)}, bf16[1568,768]{1,0:T(8,128)(2,1)S(1)}, u32[]{:S(2)}) copy-start(bf16[1568,768]{1,0:T(8,128)(2,1)S(1)} %add_convert_fusion.2) | copy-start | bytes 7225348
  83.1 11.8 %slice-start.12 = ((s8[7225344]{0:T(1024)(128)(4,1)}), s8[3031040]{0:T(1024)(128)(4,1)S(1)}, s32[]{:S(2)}) async-start(s8[7225344]{0:T(1024)(128)(4,1)} %bitcast.187), calls=%async_computation.18 | async-start | bytes 6062080
  88.0 6.9 %slice-start.13 = ((s8[7225344]{0:T(1024)(128)(4,1)}), s8[4194304]{0:T(1024)(128)(4,1)S(1)}, s32[]{:S(2)}) async-start(s8[7225344]{0:T(1024)(128)(4,1)} %bitcast.187), calls=%async_computation.19 | async-start | bytes 8388608
  102.3 7.9 %copy-start.19 = (bf16[1568,384]{1,0:T(8,128)(2,1)S(1)}, bf16[1568,384]{1,0:T(8,128)(2,1)}, u32[]{:S(2)}) copy-start(bf16[1568,384]{1,0:T(8,128)(2,1)} %get-tuple-element.146) | copy-start | bytes 3612676
  122.4 11.3 %copy-start.20 = (bf16[32,49,6,64]{3,2,1,0:T(8,128)(2,1)S(1)}, bf16[32,49,6,64]{3,2,1,0:T(8,128)(2,1)}, u32[]{:S(2)}) copy-start(bf16[32,49,6,64]{3,2,1,0:T(8,128)(2,1)} %reshape.273) | copy-start | bytes 3612676
  135.4 7.6 %copy-start.7 = (bf16[32,49,6,64]{3,2,1,0:T(8,128)(2,1)S(1)}, bf16[32,49,6,64]{3,2,1,0:T(8,128)(2,1)}, u32[]{:S(2)}) copy-start(bf16[32,49,6,64]{3,2,1,0:T(8,128)(2,1)} %reshape.280) | copy-start | bytes 3612676
  146.5 9.0 %copy-start.21 = (bf16[32,49,6,64]{3,2,1,0:T(8,128)(2,1)S(1)}, bf16[32,49,6,64]{3,2,1,0:T(8,128)(2,1)}, u32[]{:S(2)}) copy-start(bf16[32,49,6,64]{3,2,1,0:T(8,128)(2,1)} %reshape.279) | copy-start | bytes 3612676
  157.8 7.1 %copy-start.16 = (bf16[1568,384]{1,0:T(8,128)(2,1)S(1)}, bf16[1568,384]{1,0:T(8,128)(2,1)}, u32[]{:S(2)}) copy-start(bf16[1568,384]{1,0:T(8,128)(2,1)} %convert_element_type.213) | copy-start | bytes 3612676
  160.2 7.3 %slice-start = ((s8[4816896]{0:T(1024)(128)(4,1)}), s8[622592]{0:T(1024)(128)(4,1)S(1)}, s32[]{:S(2)}) async-start(s8[4816896]{0:T(1024)(128)(4,1)} %bitcast.173), calls=%async_computation.6 | async-start | bytes 1245184
  170.8 57.1 %copy-start.3 = (f32[1568,768]{1,0:T(8,128)}, f32[1568,768]{1,0:T(8,128)S(1)}, u32[]{:S(2)}) copy-start(f32[1568,768]{1,0:T(8,128)S(1)} %get-tuple-element.123) | copy-start | bytes 14450692
  174.1 8.7 %copy-start.29 = (bf16[1568,768]{1,0:T(8,128)(2,1)}, bf16[1568,768]{1,0:T(8,128)(2,1)S(1)}, u32[]{:S(2)}) copy-start(bf16[1568,768]{1,0:T(8,128)(2,1)S(1)} %add_convert_fusion.1) | copy-start | bytes 7225348
  182.9 8.8 %copy-start.14 = (bf16[1568,768]{1,0:T(8,128)(2,1)S(1)}, bf16[1568,768]{1,0:T(8,128)(2,1)}, u32[]{:S(2)}) copy-start(bf16[1568,768]{1,0:T(8,128)(2,1)} %param.26) | copy-start | bytes 7225348
  242.8 11.7 %slice-start.10 = ((s8[5505024]{0:T(1024)(128)(4,1)}), s8[1310720]{0:T(1024)(128)(4,1)S(1)}, s32[]{:S(2)}) async-start(s8[5505024]{0:T(1024)(128)(4,1)} %bitcast.184), calls=%async_computation.16 | async-start | bytes 2621440
  262.9 13.1 %slice-start.8 = ((s8[5505024]{0:T(1024)(128)(4,1)}), s8[1310720]{0:T(1024)(128)(4,1)S(1)}, s32[]{:S(2)}) async-start(s8[5505024]{0:T(1024)(128)(4,1)} %bitcast.182), calls=%async_computation.14 | async-start | bytes 2621440
  269.4 6.6 %copy-start.23 = (bf16[32,49,6,64]{3,2,1,0:T(8,128)(2,1)S(1)}, bf16[32,49,6,64]{3,2,1,0:T(8,128)(2,1)}, u32[]{:S(2)}) copy-start(bf16[32,49,6,64]{3,2,1,0:T(8,128)(2,1)} %reshape.282) | copy-start | bytes 3612676
  314.7 7.0 %copy-start.24 = (bf16[32,49,6,64]{3,1,2,0:T(8,128)(2,1)S(1)}, bf16[32,49,6,64]{3,1,2,0:T(8,128)(2,1)}, u32[]{:S(2)}) copy-start(bf16[32,49,6,64]{3,1,2,0:T(8,128)(2,1)} %get-tuple-element.139) | copy-start | bytes 3612676
  347.9 8.3 %copy-start.15 = (bf16[1568,768]{1,0:T(8,128)(2,1)S(1)}, bf16[1568,768]{1,0:T(8,128)(2,1)}, u32[]{:S(2)}) copy-start(bf16[1568,768]{1,0:T(8,128)(2,1)} %param.26) | copy-start | bytes 7225348
  347.9 247.4 %reduce-scatter.5.cloned.1.call-start = ((), (), s32[]{:S(2)}) async-start(), calls=%async_computation.5 | async-start | bytes 9732096 | tf_op jit(solution)/shard_map/reduce_scatter | solution.py:168
  348.3 18.2 %slice-start.17 = ((s8[4816896]{0:T(1024)(128)(4,1)}), s8[4194304]{0:T(1024)(128)(4,1)S(1)}, s32[]{:S(2)}) async-start(s8[4816896]{0:T(1024)(128)(4,1)} %bitcast.210), calls=%async_computation.23 | async-start | bytes 8388608
  356.2 10.3 %slice-start.18 = ((s8[4816896]{0:T(1024)(128)(4,1)}), s8[622592]{0:T(1024)(128)(4,1)S(1)}, s32[]{:S(2)}) async-start(s8[4816896]{0:T(1024)(128)(4,1)} %bitcast.210), calls=%async_computation.24 | async-start | bytes 1245184
  363.5 7.9 %slice-start.19 = ((s8[4816896]{0:T(1024)(128)(4,1)}), s8[4194304]{0:T(1024)(128)(4,1)S(1)}, s32[]{:S(2)}) async-start(s8[4816896]{0:T(1024)(128)(4,1)} %bitcast.212), calls=%async_computation.25 | async-start | bytes 8388608
  387.5 9.6 %slice-start.2 = ((s8[4816896]{0:T(1024)(128)(4,1)}), s8[622592]{0:T(1024)(128)(4,1)S(1)}, s32[]{:S(2)}) async-start(s8[4816896]{0:T(1024)(128)(4,1)} %bitcast.175), calls=%async_computation.8 | async-start | bytes 1245184
  388.8 8.3 %slice-start.3 = ((s8[4816896]{0:T(1024)(128)(4,1)}), s8[4194304]{0:T(1024)(128)(4,1)S(1)}, s32[]{:S(2)}) async-start(s8[4816896]{0:T(1024)(128)(4,1)} %bitcast.175), calls=%async_computation.9 | async-start | bytes 8388608
  388.8 8.3 %copy-start.37 = (bf16[1568,1152]{1,0:T(8,128)(2,1)S(1)}, bf16[1568,1152]{1,0:T(8,128)(2,1)}, u32[]{:S(2)}) copy-start(bf16[1568,1152]{1,0:T(8,128)(2,1)} %constant_dynamic-update-slice_fusion.3) | copy-start | bytes 10838020
  388.8 8.3 %copy-start.42 = (f32[1568]{0:T(1024)S(1)}, f32[1568]{0:T(1024)}, u32[]{:S(2)}) copy-start(f32[1568]{0:T(1024)} %copy-done.41) | copy-start | bytes 18820
  388.8 8.4 %copy-start.50 = (f32[1568]{0:T(1024)S(1)}, f32[1568]{0:T(1024)}, u32[]{:S(2)}) copy-start(f32[1568]{0:T(1024)} %copy-done.49) | copy-start | bytes 18820
  388.8 8.4 %copy-start.54 = (f32[768]{0:T(1024)S(1)}, f32[768]{0:T(1024)}, u32[]{:S(2)}) copy-start(f32[768]{0:T(1024)} %copy-done.53) | copy-start | bytes 9220
  388.8 8.4 %copy-start.58 = (bf16[1536,1152]{1,0:T(8,128)(2,1)S(1)}, bf16[1536,1152]{1,0:T(8,128)(2,1)}, u32[]{:S(2)}) copy-start(bf16[1536,1152]{1,0:T(8,128)(2,1)} %all-gather.5.cloned.1.call-done) | copy-start | bytes 10616836
  388.8 17.2 %slice-start.6 = ((s8[4816896]{0:T(1024)(128)(4,1)}), s8[4194304]{0:T(1024)(128)(4,1)S(1)}, s32[]{:S(2)}) async-start(s8[4816896]{0:T(1024)(128)(4,1)} %bitcast.179), calls=%async_computation.12 | async-start | bytes 8388608
  397.2 7.0 %copy-start.48 = (f32[1568]{0:T(1024)S(1)}, f32[1568]{0:T(1024)}, u32[]{:S(2)}) copy-start(f32[1568]{0:T(1024)} %copy-done.47) | copy-start | bytes 18820
  397.2 8.8 %slice-start.7 = ((s8[4816896]{0:T(1024)(128)(4,1)}), s8[622592]{0:T(1024)(128)(4,1)S(1)}, s32[]{:S(2)}) async-start(s8[4816896]{0:T(1024)(128)(4,1)} %bitcast.179), calls=%async_computation.13 | async-start | bytes 1245184
  406.0 10.0 %slice-start.4 = ((s8[4816896]{0:T(1024)(128)(4,1)}), s8[622592]{0:T(1024)(128)(4,1)S(1)}, s32[]{:S(2)}) async-start(s8[4816896]{0:T(1024)(128)(4,1)} %bitcast.177), calls=%async_computation.10 | async-start | bytes 1245184
  409.1 7.0 %slice-start.5 = ((s8[4816896]{0:T(1024)(128)(4,1)}), s8[4194304]{0:T(1024)(128)(4,1)S(1)}, s32[]{:S(2)}) async-start(s8[4816896]{0:T(1024)(128)(4,1)} %bitcast.177), calls=%async_computation.11 | async-start | bytes 8388608
  409.1 7.0 %copy-start.57 = (f32[768]{0:T(1024)S(1)}, f32[768]{0:T(1024)}, u32[]{:S(2)}) copy-start(f32[768]{0:T(1024)} %get-tuple-element.69) | copy-start | bytes 9220
  416.1 228.1 %copy-start.44 = (f32[6,768]{1,0:T(8,128)S(1)}, f32[6,768]{1,0:T(8,128)}, u32[]{:S(2)}) copy-start(f32[6,768]{1,0:T(8,128)} %param.43) | copy-start | bytes 55300
  416.1 229.5 %copy-start.40 = (f32[384,48]{0,1:T(8,128)S(1)}, f32[384,48]{0,1:T(8,128)}, u32[]{:S(2)}) copy-start(f32[384,48]{0,1:T(8,128)} %param.31) | copy-start | bytes 221188
  424.8 222.4 %copy-start.52 = (f32[6,384]{1,0:T(8,128)S(1)}, f32[6,384]{1,0:T(8,128)}, u32[]{:S(2)}) copy-start(f32[6,384]{1,0:T(8,128)} %param.40) | copy-start | bytes 27652
  424.8 223.8 %copy-start.34 = (f32[48,3,384]{2,0,1:T(8,128)S(1)}, f32[48,3,384]{2,0,1:T(8,128)}, u32[]{:S(2)}) copy-start(f32[48,3,384]{2,0,1:T(8,128)} %param.28) | copy-start | bytes 663556
  424.8 225.7 %copy-start.32 = (f32[48,4,384]{2,1,0:T(4,128)S(1)}, f32[48,4,384]{2,1,0:T(4,128)}, u32[]{:S(2)}) copy-start(f32[48,4,384]{2,1,0:T(4,128)} %param.34) | copy-start | bytes 884740
  424.8 225.7 %copy-start.38 = (f32[48,4,384]{2,1,0:T(4,128)S(1)}, f32[48,4,384]{2,1,0:T(4,128)}, u32[]{:S(2)}) copy-start(f32[48,4,384]{2,1,0:T(4,128)} %param.36) | copy-start | bytes 884740
  424.8 225.7 %copy-start.39 = (f32[48,4,384]{2,1,0:T(4,128)S(1)}, f32[48,4,384]{2,1,0:T(4,128)}, u32[]{:S(2)}) copy-start(f32[48,4,384]{2,1,0:T(4,128)} %param.35) | copy-start | bytes 884740
  424.8 227.0 %copy-start.33 = (f32[4,384,48]{1,2,0:T(8,128)S(1)}, f32[4,384,48]{1,2,0:T(8,128)}, u32[]{:S(2)}) copy-start(f32[4,384,48]{1,2,0:T(8,128)} %param.37) | copy-start | bytes 884740
  642.9 11.1 %copy-start.1 = (f32[196,768]{1,0:T(8,128)S(1)}, f32[196,768]{1,0:T(8,128)}, u32[]{:S(2)}) copy-start(f32[196,768]{1,0:T(8,128)} %param.25) | copy-start | bytes 1806340
  (37 other events, 134.0 us)
Sparse Core Ops, SparseCore 0:
  11.5 62.6 all-gather.4
  77.1 85.3 all-gather.6
  348.0 106.2 reduce-scatter.2
  460.1 135.1 reduce-scatter.4
where the time goes:
time: 673 us; the launch traced here: 662 us
  waiting for transfers between devices  209 us (31%)
  matrix products  193 us (29%)
  local copies, waits for them, and re-layouts  116 us (17%)
  other arithmetic  76.6 us (11%)
  blocking collectives  46 us (7%)
  between operations  20.5 us (3%)
    reduce_scatter x2, waiting for transfers between devices, scatter(): lax.psum_scatter(stacked, every, scatter_dimension=0, tiled=True)  169 us
    dot_general x8, matrix products, dot_back(): lax.dot_general(left_side, right_side, (((1,), (1,)), ((), ())), preferre...  52.4 us
    dot_general x8, matrix products, transpose_dot(): lax.dot_general(left_side, right_side, (((0,), (0,)), ((), ())), preferre...  42.7 us
    psum x1, blocking collectives, body(): lax.psum((grad_norm_rows, grad_split, local_square), ('dp', 'tensor'))  40.4 us
    all_gather x2, waiting for transfers between devices, gather(): whole = lax.all_gather(block.astype(low_type), every, axis=0, tiled=True)  40.4 us
    unnamed x167, local copies, waits for them, and re-layouts  22.2 us
    dot_general x2, matrix products, body(): jnp.dot(cotangent, fc2_low[t], preferred_element_type=jnp.float32)  20.5 us
    sub x2, other arithmetic, body(): attention = jax.nn.softmax(scores, axis=-1)  17.9 us
  transfers between devices with their start and end apart: 4, of which 3 were waited for; matrix products, arithmetic and copies ran while one was open for 27% of the time, Pallas kernels for 0%

commit v1 on v0

--- a/solution.py
+++ b/solution.py
@@ -96,7 +96,9 @@
         return jnp.swapaxes(proj_like, -1, -2)
 
     def gather(block):
-        whole = lax.all_gather(block.astype(low_type), every, axis=0, tiled=True)
+        block_2 = block.astype(low_type)
+        sent = jnp.stack([block_2] * lax.axis_size(every))
+        whole = jnp.concatenate(lax.all_to_all(sent, every, 0, 0), axis=0)
         return whole.reshape(halves, model_width, block.shape[1])
 
     fc2_rows = jnp.transpose(w_fc2, (2, 0, 1)).reshape(shard_rows, 4 * shard_width)

time: 673 us -> 857 us (1.27)
  waiting for transfers between devices: 209 us -> 312 us
  blocking collectives: 46 us -> 109 us
  starting transfers between devices: 0.57 us -> 11.6 us
  local copies, waits for them, and re-layouts: 116 us -> 125 us
    all_to_all x0 -> x2, waiting for transfers between devices: none -> 144 us  [gather(): whole = jnp.concatenate(lax.all_to_all(sent, every, 0, 0), axis=0)]
    all_gather x1, blocking collectives: 5.6 us -> 68.9 us  [body(): split_whole_bias = lax.all_gather(split_bias, 'tensor', axis=0, tiled=False)]
    all_gather x2 -> x0, waiting for transfers between devices: 40.4 us -> none  [gather(): whole = lax.all_gather(block.astype(low_type), every, axis=0, tiled=True)]
    all_to_all x0 -> x2, starting transfers between devices: none -> 11.3 us  [gather(): whole = jnp.concatenate(lax.all_to_all(sent, every, 0, 0), axis=0)]
    unnamed x167 -> x169, local copies, waits for them, and re-layouts: 22.2 us -> 12.5 us
  transfers between devices with their start and end apart: 4 -> 4, of which waited for: 3 -> 4; matrix products, arithmetic and copies ran while one was open for 27% -> 20% of each run, Pallas kernels for 0% -> 0%
where the time goes in v1:
time: 857 us; the launch traced here: 845 us
  waiting for transfers between devices  312 us (36%)
  matrix products  191 us (22%)
  local copies, waits for them, and re-layouts  125 us (15%)
  blocking collectives  109 us (13%)
  other arithmetic  75.2 us (9%)
  between operations  21.2 us (2%)
  starting transfers between devices  11.6 us (1%)
    reduce_scatter x2, waiting for transfers between devices, scatter(): lax.psum_scatter(stacked, every, scatter_dimension=0, tiled=True)  168 us
    all_to_all x2, waiting for transfers between devices, gather(): whole = jnp.concatenate(lax.all_to_all(sent, every, 0, 0), axis=0)  144 us
    all_gather x1, blocking collectives, body(): split_whole_bias = lax.all_gather(split_bias, 'tensor', axis=0, tiled=False)  68.9 us
    dot_general x8, matrix products, dot_back(): lax.dot_general(left_side, right_side, (((1,), (1,)), ((), ())), preferre...  52.9 us
    dot_general x8, matrix products, transpose_dot(): lax.dot_general(left_side, right_side, (((0,), (0,)), ((), ())), preferre...  41.9 us
    psum x1, blocking collectives, body(): lax.psum((grad_norm_rows, grad_split, local_square), ('dp', 'tensor'))  40.4 us
    dot_general x2, matrix products, body(): jnp.dot(cotangent, fc2_low[t], preferred_element_type=jnp.float32)  20.5 us
    dot_general x2, matrix products, body(): jnp.dot(normed_two_low, fc1_low[t], preferred_element_type=jnp.float32)  18 us
  transfers between devices with their start and end apart: 4, of which 4 were waited for; matrix products, arithmetic and copies ran while one was open for 20% of the time, Pallas kernels for 0%

profile of v1, /device:TPU:0, one launch (start us, length us, event | category | flops | bytes accessed | tf_op | source)
XLA Modules:
  0.0 845.4 jit_solution(16880304775108819399)
XLA Ops:
  10.3 7.4 all-to-all-start
  18.0 80.6 %all-to-all-done = bf16[32,48,1152]{2,1,0:T(8,128)(2,1)} async-done(((bf16[32,48,1152]{2,1,0:T(8,128)(2,1)}), bf16[32,48,1152]{2,1,0:T(8,128)(2,1)}, u32[]{:S(2)}, u32[]{:S(2)}) %all-to-all-start) | async-done | bytes 3538976 | tf_op jit(solution)/shard_map/all_to_all | solution.py:101
  98.5 4.6 stack.37
  107.3 68.9 %all-gather.1 = f32[2,6,384]{2,1,0:T(8,128)S(1)} all-gather(f32[1,6,384]{2,1,0:T(8,128)S(1)} %bitcast.203), channel_id=2, replica_groups=mesh['dp'=16,'tensor'=2] {'tensor'}, dimensions={0}, use_global_device_ids=true | all-gather | bytes 27648 | tf_op jit(solution)/shard_map/all_gather | solution.py:114
  176.3 6.1 gather_fusion
  188.9 4.4 fusion.101
  202.9 5.7 fusion.106
  211.1 4.7 reshape.284
  219.0 4.8 reshape.283
  230.3 4.5 fusion.53
  234.8 8.9 %fusion.103 = (f32[32,6,49]{2,1,0:T(8,128)S(1)}, f32[32,6,49,49]{2,3,1,0:T(8,128)S(1)}) fusion(f32[32,6,49,49]{2,3,1,0:T(8,128)S(1)} %fusion.53), kind=kOutput, calls=%fused_computation.225 | output fusion | flops 1844016 | bytes 3725568 | tf_op jit(solution)/shard_map/sub | solution.py:136
  248.5 4.3 convert_element_type.217
  252.8 4.5 fusion.45
  257.3 8.9 %fusion.104 = (f32[32,6,49]{2,1,0:T(8,128)S(1)}, f32[32,6,49,49]{2,3,1,0:T(8,128)S(1)}) fusion(f32[32,6,49,49]{2,3,1,0:T(8,128)S(1)} %fusion.45), kind=kOutput, calls=%fused_computation.226 | output fusion | flops 1844016 | bytes 3725568 | tf_op jit(solution)/shard_map/sub | solution.py:136
  271.0 5.4 convert_element_type.223
  276.4 63.4 %all-to-all-done.1 = bf16[32,48,3456]{2,1,0:T(8,128)(2,1)} async-done(((bf16[32,48,3456]{2,1,0:T(8,128)(2,1)}), bf16[32,48,3456]{2,1,0:T(8,128)(2,1)}, u32[]{:S(2)}, u32[]{:S(2)}) %all-to-all-start.1) | async-done | bytes 10616864 | tf_op jit(solution)/shard_map/all_to_all | solution.py:101
  347.5 8.5 %multiply_convert_fusion = (bf16[1568,1536]{1,0:T(8,128)(2,1)}, f32[1568,1536]{1,0:T(8,128)S(1)}) fusion(f32[1536]{0:T(1024)S(1)} %add.329, bf16[1568,768]{1,0:T(8,128)(2,1)S(1)} %add_convert_fusion.1, bf16[2,768,3456]{2,1,0:T(8,128)(2,1)} %bitcast.5), kind=kOutput, calls=%fused_computation.21 | convolution fusion | flops 3713826816 | bytes 19224576 | tf_op jit(solution)/shard_map/dot_general | solution.py:153
  356.0 9.5 %multiply_convert_fusion.1 = (bf16[1568,1536]{1,0:T(8,128)(2,1)}, f32[1568,1536]{1,0:T(8,128)}) fusion(f32[1536]{0:T(1024)S(1)} %add.325, bf16[1568,768]{1,0:T(8,128)(2,1)S(1)} %add_convert_fusion.1, bf16[2,768,3456]{2,1,0:T(8,128)(2,1)} %bitcast.5), kind=kOutput, calls=%fused_computation.23 | convolution fusion | flops 3713826816 | bytes 19224576 | tf_op jit(solution)/shard_map/dot_general | solution.py:153
  365.5 10.3 %convert_reduce_fusion = (f32[1536]{0:T(1024)}, bf16[1568,1536]{1,0:T(8,128)(2,1)}) fusion(f32[1568,1536]{1,0:T(8,128)S(1)} %get-tuple-element.129, bf16[1568,768]{1,0:T(8,128)(2,1)S(1)} %copy-done.12, bf16[2,768,3456]{2,1,0:T(8,128)(2,1)} %bitcast.5), kind=kOutput, calls=%fused_computation.19 | convolution fusion | flops 3733092864 | bytes 19224576 | tf_op jit(solution)/shard_map/dot_general | solution.py:161
  375.9 10.1 %convert_reduce_fusion.1 = (f32[1536]{0:T(1024)}, bf16[1568,1536]{1,0:T(8,128)(2,1)S(1)}) fusion(f32[1568,1536]{1,0:T(8,128)} %get-tuple-element.127, bf16[1568,768]{1,0:T(8,128)(2,1)S(1)} %copy-done.12, bf16[2,768,3456]{2,1,0:T(8,128)(2,1)} %bitcast.5), kind=kOutput, calls=%fused_computation.20 | convolution fusion | flops 3733092864 | bytes 19224576 | tf_op jit(solution)/shard_map/dot_general | solution.py:161
  386.0 8.9 %fusion.65 = f32[1568,768]{1,0:T(8,128)} fusion(bf16[1568,1536]{1,0:T(8,128)(2,1)S(1)} %get-tuple-element.143, bf16[2,768,3456]{2,1,0:T(8,128)(2,1)} %bitcast.5), kind=kOutput, calls=%fused_computation.131 | convolution fusion | flops 3699376128 | bytes 11993088 | tf_op jit(solution)/shard_map/dot_general | solution.py:43
  394.9 9.9 %multiply_reduce_fusion.4 = (f32[768]{0:T(1024)S(1)}, f32[1568]{0:T(1024)S(1)}, f32[768]{0:T(1024)S(1)}, f32[1568,768]{1,0:T(8,128)S(1)}) fusion(f32[1568,768]{1,0:T(8,128)S(1)} %get-tuple-element.125, f32[1568]{0:T(1024)S(1)} %fusion.84, f32[1568]{0:T(1024)S(1)} %broadcast_multiply_fusion, f32[768]{0:T(1024)S(1)} %get-tuple-element.71, ...), kind=kOutput, calls=%fused_computation.50 | convolution fusion | flops 3710211072 | bytes 21654912 | tf_op jit(solution)/shard_map/dot_general | solution.py:43
  419.0 5.0 reshape.290
  424.0 6.5 multiply_reduce_fusion
  445.4 6.5 multiply_reduce_fusion.1
  464.5 5.2 reshape.292
  472.0 4.3 reshape.288
  480.4 4.7 reshape.287
  486.3 4.1 copy.187
  490.4 4.3 reshape.289
  497.2 7.0 convolution_convert_fusion.1
  506.5 4.3 reshape.291
  512.1 4.2 copy.196
  516.2 4.3 reshape.293
  523.0 5.9 convolution_convert_fusion
  532.1 7.8 convolution_convert_fusion.3
  539.9 7.3 fusion.22
  550.2 4.8 convolution_convert_fusion.5
  555.1 5.0 fusion.21
  562.8 8.4 pad_maximum_fusion
  572.8 5.6 fusion.108
  578.5 6.8 multiply_reduce_fusion.5
  585.3 4.3 fusion.98
  592.7 7.0 fusion.66
  599.8 9.0 %add_convert_fusion = bf16[1568,768]{1,0:T(8,128)(2,1)} fusion(f32[1568,768]{1,0:T(8,128)S(1)} %bitcast.184, f32[1568,768]{1,0:T(8,128)S(1)} %fusion.66, bf16[1568,1536]{1,0:T(8,128)(2,1)} %get-tuple-element.128, f32[768]{0:T(1024)S(1)} %copy-done.64, bf16[2,768,3456]{2,1,0:T(8,128)(2,1)} %bitcast.5), kind=kOutput, calls=%fused_computation.56 | convolution fusion | flops 3704193024 | bytes 19221504 | tf_op jit(solution)/shard_map/dot_general | solution.py:43
  608.8 28.4 %reduce-scatter.3.cloned.1.call-done = bf16[48,1536]{1,0:T(8,128)(2,1)} async-done(((bf16[1536,1536]{1,0:T(8,128)(2,1)}), bf16[48,1536]{1,0:T(8,128)(2,1)}) %reduce-scatter.3.cloned.1.call-update) | async-done | bytes 147472 | tf_op jit(solution)/shard_map/reduce_scatter | solution.py:170
  638.8 139.5 %reduce-scatter.5.cloned.1.call-done = bf16[48,3072]{1,0:T(8,128)(2,1)} async-done(((bf16[1536,3072]{1,0:T(8,128)(2,1)}), bf16[48,3072]{1,0:T(8,128)(2,1)}) %reduce-scatter.5.cloned.1.call-update) | async-done | bytes 294928 | tf_op jit(solution)/shard_map/reduce_scatter | solution.py:170
  782.3 40.4 %all-reduce = (f32[]{:T(128)}, f32[6,768]{1,0:T(8,128)S(1)}, f32[2,6,384]{2,1,0:T(8,128)S(1)}) all-reduce(f32[]{:T(128)S(6)} %add.344, f32[6,768]{1,0:T(8,128)S(1)} %stack.46, f32[2,6,384]{2,1,0:T(8,128)S(1)} %pad_maximum_fusion.3), channel_id=1, replica_groups=mesh['dp'=16,'tensor'=2] {'dp','tensor'}, use_global_device_ids=true, to_apply=%region_18.19 | all-reduce | flops 9217 | bytes 73736 | tf_op jit(solution)/shard_map/psum | solution.py:250
  (285 shorter events, 138.9 us)
Async XLA Ops:
  7.2 169.1 %copy-start = (f32[196,768]{1,0:T(8,128)S(1)}, f32[196,768]{1,0:T(8,128)}, u32[]{:S(2)}) copy-start(f32[196,768]{1,0:T(8,128)} %param.25) | copy-start | bytes 1806340
  8.2 9.5 %copy-start.35 = (f32[48,4,384]{2,1,0:T(4,128)S(1)}, f32[48,4,384]{2,1,0:T(4,128)}, u32[]{:S(2)}) copy-start(f32[48,4,384]{2,1,0:T(4,128)} %param.34) | copy-start | bytes 884740
  10.3 7.6 copy-start.37
  10.3 7.6 copy-start.44
  10.3 88.2 %all-to-all-start = ((bf16[32,48,1152]{2,1,0:T(8,128)(2,1)}), bf16[32,48,1152]{2,1,0:T(8,128)(2,1)}, u32[]{:S(2)}, u32[]{:S(2)}) async-start(bf16[32,48,1152]{2,1,0:T(8,128)(2,1)} %stack.36), calls=%async_computation | async-start | bytes 7077888 | tf_op jit(solution)/shard_map/all_to_all | solution.py:101
  103.2 236.7 %all-to-all-start.1 = ((bf16[32,48,3456]{2,1,0:T(8,128)(2,1)}), bf16[32,48,3456]{2,1,0:T(8,128)(2,1)}, u32[]{:S(2)}, u32[]{:S(2)}) async-start(bf16[32,48,3456]{2,1,0:T(8,128)(2,1)} %stack.37), calls=%async_computation.1 | async-start | bytes 21233664 | tf_op jit(solution)/shard_map/all_to_all | solution.py:101
  107.0 530.2 %reduce-scatter.3.cloned.1.call-start = ((), (), s32[]{:S(2)}) async-start(), calls=%async_computation.4 | async-start | bytes 4866048 | tf_op jit(solution)/shard_map/reduce_scatter | solution.py:170
  176.3 6.2 copy-start.48
  176.3 6.8 copy-start.25
  188.9 7.7 copy-start.26
  234.8 9.0 %copy-start.20 = (bf16[32,49,6,64]{3,2,1,0:T(8,128)(2,1)S(1)}, bf16[32,49,6,64]{3,2,1,0:T(8,128)(2,1)}, u32[]{:S(2)}) copy-start(bf16[32,49,6,64]{3,2,1,0:T(8,128)(2,1)} %reshape.280) | copy-start | bytes 3612676
  257.3 9.0 %copy-start.21 = (bf16[32,49,6,64]{3,2,1,0:T(8,128)(2,1)S(1)}, bf16[32,49,6,64]{3,2,1,0:T(8,128)(2,1)}, u32[]{:S(2)}) copy-start(bf16[32,49,6,64]{3,2,1,0:T(8,128)(2,1)} %reshape.283) | copy-start | bytes 3612676
  271.0 71.5 %slice-start = ((s8[4816896]{0:T(1024)(128)(4,1)}), s8[622592]{0:T(1024)(128)(4,1)S(1)}, s32[]{:S(2)}) async-start(s8[4816896]{0:T(1024)(128)(4,1)} %bitcast.179), calls=%async_computation.6 | async-start | bytes 1245184
  345.6 59.3 %copy-start.3 = (f32[1568,768]{1,0:T(8,128)}, f32[1568,768]{1,0:T(8,128)S(1)}, u32[]{:S(2)}) copy-start(f32[1568,768]{1,0:T(8,128)S(1)} %get-tuple-element.125) | copy-start | bytes 14450692
  347.5 8.5 %copy-start.29 = (bf16[1568,768]{1,0:T(8,128)(2,1)}, bf16[1568,768]{1,0:T(8,128)(2,1)S(1)}, u32[]{:S(2)}) copy-start(bf16[1568,768]{1,0:T(8,128)(2,1)S(1)} %add_convert_fusion.1) | copy-start | bytes 7225348
  356.0 9.5 %copy-start.12 = (bf16[1568,768]{1,0:T(8,128)(2,1)S(1)}, bf16[1568,768]{1,0:T(8,128)(2,1)}, u32[]{:S(2)}) copy-start(bf16[1568,768]{1,0:T(8,128)(2,1)} %param.26) | copy-start | bytes 7225348
  386.0 8.9 %copy-start.65 = (bf16[1568,1536]{1,0:T(8,128)(2,1)}, bf16[1568,1536]{1,0:T(8,128)(2,1)S(1)}, u32[]{:S(2)}) copy-start(bf16[1568,1536]{1,0:T(8,128)(2,1)S(1)} %get-tuple-element.143) | copy-start | bytes 14450692
  419.0 11.5 %slice-start.10 = ((s8[5505024]{0:T(1024)(128)(4,1)}), s8[1310720]{0:T(1024)(128)(4,1)S(1)}, s32[]{:S(2)}) async-start(s8[5505024]{0:T(1024)(128)(4,1)} %bitcast.190), calls=%async_computation.16 | async-start | bytes 2621440
  424.0 6.5 slice-start.11
  424.0 6.6 copy-start.22
  438.7 13.1 %slice-start.8 = ((s8[5505024]{0:T(1024)(128)(4,1)}), s8[1310720]{0:T(1024)(128)(4,1)S(1)}, s32[]{:S(2)}) async-start(s8[5505024]{0:T(1024)(128)(4,1)} %bitcast.188), calls=%async_computation.14 | async-start | bytes 2621440
  445.4 6.5 slice-start.9
  445.4 6.6 copy-start.23
  497.2 7.0 copy-start.24
  512.1 8.5 %copy-start.18 = (bf16[1568,384]{1,0:T(8,128)(2,1)S(1)}, bf16[1568,384]{1,0:T(8,128)(2,1)}, u32[]{:S(2)}) copy-start(bf16[1568,384]{1,0:T(8,128)(2,1)} %reshape.292) | copy-start | bytes 3612676
  523.0 6.0 copy-start.34
  523.0 6.0 copy-start.40
  531.8 8.0 copy-start.13
  531.9 246.5 %reduce-scatter.5.cloned.1.call-start = ((), (), s32[]{:S(2)}) async-start(), calls=%async_computation.5 | async-start | bytes 9732096 | tf_op jit(solution)/shard_map/reduce_scatter | solution.py:170
  532.1 18.1 %slice-start.12 = ((s8[4816896]{0:T(1024)(128)(4,1)}), s8[4194304]{0:T(1024)(128)(4,1)S(1)}, s32[]{:S(2)}) async-start(s8[4816896]{0:T(1024)(128)(4,1)} %bitcast.204), calls=%async_computation.18 | async-start | bytes 8388608
  539.9 10.3 %slice-start.13 = ((s8[4816896]{0:T(1024)(128)(4,1)}), s8[622592]{0:T(1024)(128)(4,1)S(1)}, s32[]{:S(2)}) async-start(s8[4816896]{0:T(1024)(128)(4,1)} %bitcast.204), calls=%async_computation.19 | async-start | bytes 1245184
  547.2 7.9 slice-start.14
  571.3 7.1 slice-start.2
  572.8 16.8 %slice-start.6 = ((s8[4816896]{0:T(1024)(128)(4,1)}), s8[4194304]{0:T(1024)(128)(4,1)S(1)}, s32[]{:S(2)}) async-start(s8[4816896]{0:T(1024)(128)(4,1)} %bitcast.185), calls=%async_computation.12 | async-start | bytes 8388608
  578.5 6.8 copy-start.53
  578.5 11.2 %slice-start.7 = ((s8[4816896]{0:T(1024)(128)(4,1)}), s8[622592]{0:T(1024)(128)(4,1)S(1)}, s32[]{:S(2)}) async-start(s8[4816896]{0:T(1024)(128)(4,1)} %bitcast.185), calls=%async_computation.13 | async-start | bytes 1245184
  589.7 10.0 %slice-start.4 = ((s8[4816896]{0:T(1024)(128)(4,1)}), s8[622592]{0:T(1024)(128)(4,1)S(1)}, s32[]{:S(2)}) async-start(s8[4816896]{0:T(1024)(128)(4,1)} %bitcast.183), calls=%async_computation.10 | async-start | bytes 1245184
  592.7 7.1 slice-start.5
  592.7 7.1 copy-start.64
  599.8 227.5 %copy-start.49 = (f32[6,768]{1,0:T(8,128)S(1)}, f32[6,768]{1,0:T(8,128)}, u32[]{:S(2)}) copy-start(f32[6,768]{1,0:T(8,128)} %param.43) | copy-start | bytes 55300
  599.8 228.9 %copy-start.45 = (f32[384,48]{0,1:T(8,128)S(1)}, f32[384,48]{0,1:T(8,128)}, u32[]{:S(2)}) copy-start(f32[384,48]{0,1:T(8,128)} %param.31) | copy-start | bytes 221188
  608.8 221.5 %copy-start.59 = (f32[6,384]{1,0:T(8,128)S(1)}, f32[6,384]{1,0:T(8,128)}, u32[]{:S(2)}) copy-start(f32[6,384]{1,0:T(8,128)} %param.40) | copy-start | bytes 27652
  608.8 222.9 %copy-start.39 = (f32[48,3,384]{2,0,1:T(8,128)S(1)}, f32[48,3,384]{2,0,1:T(8,128)}, u32[]{:S(2)}) copy-start(f32[48,3,384]{2,0,1:T(8,128)} %param.28) | copy-start | bytes 663556
  608.8 224.9 %copy-start.36 = (f32[48,4,384]{2,1,0:T(4,128)S(1)}, f32[48,4,384]{2,1,0:T(4,128)}, u32[]{:S(2)}) copy-start(f32[48,4,384]{2,1,0:T(4,128)} %param.34) | copy-start | bytes 884740
  608.8 224.9 %copy-start.42 = (f32[48,4,384]{2,1,0:T(4,128)S(1)}, f32[48,4,384]{2,1,0:T(4,128)}, u32[]{:S(2)}) copy-start(f32[48,4,384]{2,1,0:T(4,128)} %param.36) | copy-start | bytes 884740
  608.8 224.8 %copy-start.43 = (f32[48,4,384]{2,1,0:T(4,128)S(1)}, f32[48,4,384]{2,1,0:T(4,128)}, u32[]{:S(2)}) copy-start(f32[48,4,384]{2,1,0:T(4,128)} %param.35) | copy-start | bytes 884740
  608.8 226.2 %copy-start.38 = (f32[4,384,48]{1,2,0:T(8,128)S(1)}, f32[4,384,48]{1,2,0:T(8,128)}, u32[]{:S(2)}) copy-start(f32[4,384,48]{1,2,0:T(8,128)} %param.37) | copy-start | bytes 884740
  826.0 11.1 %copy-start.1 = (f32[196,768]{1,0:T(8,128)S(1)}, f32[196,768]{1,0:T(8,128)}, u32[]{:S(2)}) copy-start(f32[196,768]{1,0:T(8,128)} %param.25) | copy-start | bytes 1806340
  (38 other events, 135.1 us)
Sparse Core Ops, SparseCore 0:
  532.0 105.2 reduce-scatter.2
  643.1 135.1 reduce-scatter.4
